TPU v7x, 512 devices: a whole 4x8x8 slice. The times are simulated.
512 devices in a mesh: freq: 128 (over z, y, core), panel: 4 (over x).
Axes of the slice: x: 4, y: 8, z: 8, core: 2. Of those that a mesh axis runs over, the one named last changes fastest.
Arguments:
- wave: bfloat16 [2, 128, 1600, 1600], P(None, 'freq', 'panel'), may hold values from -0.15625 to 0.15625
- observed: float32 [4, 6400, 512], P('panel', 'freq'), may hold values from -25 to 25
Outputs:
- solution: float32 [25600, 512], P('freq')
All inputs are finite; a program needn't handle non-finite values.
Results may differ from a plain program's by a relative error of at most 0.0085.
Values may be sent and summed in bfloat16 or wider, within the bound.
A program may use at most 64 MiB of HBM per device.

v0:
```python
import math
import jax
import jax.numpy as jnp
from jax import lax
from jax.sharding import PartitionSpec as P

VS = 16
ITERS = 3
precise = lax.Precision.HIGHEST
epsilon = 1e-06


def transform_tables(freq_total, samples):
    freq_index = lax.broadcasted_iota(jnp.int32, (freq_total, samples), 0) + 1
    time_index = lax.broadcasted_iota(jnp.int32, (freq_total, samples), 1)
    phases = (freq_index * time_index % samples).astype(jnp.float32) * (2.0 * math.pi / samples)
    factor = math.sqrt(2.0 / samples)
    return jnp.stack([factor * jnp.cos(phases), -factor * jnp.sin(phases)])


def spectrum_flat(rows, table):
    return jnp.einsum("cft,rt->fcr", table, rows, precision=precise).reshape(-1)


def owner_layout(received, blocks, local_freqs):
    pieces = received.reshape(blocks, local_freqs, 2, -1).transpose(2, 1, 0, 3)
    return pieces.reshape(2, local_freqs, -1)


def trace_layout(spectrum, blocks):
    parts, local_freqs, total_rows = spectrum.shape
    pieces = spectrum.reshape(parts, local_freqs, blocks, total_rows // blocks).transpose(
        2, 1, 0, 3
    )
    return pieces.reshape(-1)


def time_traces(received, table, blocks, local_freqs):
    pieces = received.reshape(blocks, local_freqs, 2, -1).astype(jnp.float32)
    folded = table.reshape(2, blocks, local_freqs, table.shape[2])
    return jnp.einsum("jlcr,cjlt->rt", pieces, folded, precision=precise)


def forward_product(spectrum, wave):

    def product_of(left, right):
        return jnp.einsum("fvs,frs->fvr", left, right, preferred_element_type=jnp.float32)

    real_out = product_of(spectrum[0], wave[0]) - product_of(spectrum[1], wave[1])
    imag_out = product_of(spectrum[0], wave[1]) + product_of(spectrum[1], wave[0])
    return jnp.stack([real_out, imag_out]).astype(jnp.bfloat16)


def adjoint_product(spectrum, wave):

    def product_of(left, right):
        return jnp.einsum("fvr,frs->fvs", left, right, preferred_element_type=jnp.float32)

    real_out = product_of(spectrum[0], wave[0]) + product_of(spectrum[1], wave[1])
    imag_out = product_of(spectrum[1], wave[0]) - product_of(spectrum[0], wave[1])
    return jnp.stack([real_out, imag_out])


def on_device(wave, observed):
    local_freqs = wave.shape[1]
    panel_rows = wave.shape[2]
    blocks = lax.axis_size("freq")
    freq_total = local_freqs * blocks
    samples = observed.shape[2]
    table = transform_tables(freq_total, samples)

    def summed_panels(partial_sum):
        return lax.psum(partial_sum, "panel")

    def adjoint(data):
        lines = spectrum_flat(data, table).astype(jnp.bfloat16)
        moved_in = lax.all_to_all(lines, "freq", split_axis=0, concat_axis=0, tiled=True)
        spectrum = owner_layout(moved_in, blocks, local_freqs).reshape(
            2, local_freqs, VS, panel_rows
        )
        partial_sum = adjoint_product(spectrum, wave)
        total = summed_panels(partial_sum).reshape(2, local_freqs, -1)
        moved = lax.all_to_all(
            trace_layout(total, blocks), "freq", split_axis=0, concat_axis=0, tiled=True
        )
        return time_traces(moved, table, blocks, local_freqs)

    def data_norm(field):
        return jnp.sqrt(lax.psum(jnp.sum(field * field), ("freq", "panel")) + epsilon)

    def model_norm(field):
        return jnp.sqrt(lax.psum(jnp.sum(field * field), "freq") + epsilon)

    data_vector = observed[0]
    beta = data_norm(data_vector)
    data_vector = data_vector / beta
    model_vector = adjoint(data_vector)
    alpha = model_norm(model_vector)
    model_vector = model_vector / alpha
    direction = model_vector
    solution = jnp.zeros_like(model_vector)
    phi_bar = beta
    rho_bar = alpha
    for step in range(ITERS):
        forward_lines = spectrum_flat(model_vector, table).astype(jnp.bfloat16)
        forward_moved_in = lax.all_to_all(
            forward_lines, "freq", split_axis=0, concat_axis=0, tiled=True
        )
        forward_spectrum = owner_layout(forward_moved_in, blocks, local_freqs).reshape(
            2, local_freqs, VS, -1
        )
        product = forward_product(forward_spectrum, wave).reshape(2, local_freqs, -1)
        forward_moved = lax.all_to_all(
            trace_layout(product, blocks), "freq", split_axis=0, concat_axis=0, tiled=True
        )
        data_vector = time_traces(forward_moved, table, blocks, local_freqs) - alpha * data_vector
        beta = data_norm(data_vector)
        data_vector = data_vector / beta
        model_vector = adjoint(data_vector) - beta * model_vector
        alpha = model_norm(model_vector)
        model_vector = model_vector / alpha
        rho_new = jnp.sqrt(rho_bar * rho_bar + beta * beta)
        cosine = rho_bar / rho_new
        sine_part = beta / rho_new
        theta = sine_part * alpha
        rho_bar = -cosine * alpha
        phi_value = cosine * phi_bar
        phi_bar = sine_part * phi_bar
        solution = solution + phi_value / rho_new * direction
        direction = model_vector - theta / rho_new * direction
    return solution


def solution(mesh):
    placed = (P(None, "freq", "panel", None), P("panel", "freq", None))
    return jax.shard_map(
        on_device, mesh=mesh, in_specs=placed, out_specs=P("freq", None), check_vma=False
    )
```

profile of v0, /device:TPU:1, one launch (start us, length us, event | category | flops | bytes accessed | tf_op | source)
XLA Modules:
  0.0 1600.5 jit_solution(7903671710847964002)
XLA Ops:
  6.5 1.9 multiply_reduce_fusion.5
  8.4 106.0 %psum.70 = f32[]{:T(128)} all-reduce(f32[]{:T(128)} %multiply_reduce_fusion.5), channel_id=1, replica_groups=mesh['freq'=128,'panel'=4] {'freq','panel'}, use_global_device_ids=true, to_apply=%region_1.2 | all-reduce | flops 1 | bytes 8 | tf_op jit(solution)/shard_map/psum | solution.py:89
  118.6 20.5 %all_to_all.90 = bf16[128,100,1]{1,2,0:T(2,128)(2,1)S(1)} all-to-all(bf16[128,100,1]{1,2,0:T(2,128)(2,1)S(1)} %copy.37), channel_id=1, replica_groups=mesh['freq'=128,'panel'=4] {'freq'}, dimensions={0} | all-to-all | bytes 51200 | tf_op jit(solution)/shard_map/all_to_all | solution.py:77
  143.3 40.2 %all-reduce.4.cloned.1.call-done = f32[128,400,1]{0,1,2:T(8,128)} async-done(((f32[128,400,1]{0,1,2:T(8,128)}), f32[128,400,1]{0,1,2:T(8,128)}) %all-reduce.4.cloned.1.call-update) | async-done | bytes 204816 | tf_op jit(solution)/shard_map/psum | solution.py:73
  184.6 31.3 %all_to_all.91 = f32[128,400,1]{1,2,0:T(1,128)S(1)} all-to-all(f32[128,400,1]{1,2,0:T(1,128)S(1)} %copy.42), channel_id=1, replica_groups=mesh['freq'=128,'panel'=4] {'freq'}, dimensions={0} | all-to-all | bytes 409600 | tf_op jit(solution)/shard_map/all_to_all | solution.py:83
  216.0 2.2 multiply_reduce_fusion.2
  218.3 247.2 %psum.72 = f32[]{:T(128)} all-reduce(f32[]{:T(128)} %get-tuple-element.19), channel_id=1, replica_groups=mesh['freq'=128,'panel'=4] {'freq'}, use_global_device_ids=true, to_apply=%region_4.5 | all-reduce | flops 1 | bytes 8 | tf_op jit(solution)/shard_map/psum | solution.py:92
  470.3 19.2 %all_to_all.92 = bf16[128,2,200]{2,1,0:T(2,128)(2,1)S(1)} all-to-all(bf16[128,2,200]{2,1,0:T(2,128)(2,1)S(1)} %reshape.643), channel_id=1, replica_groups=mesh['freq'=128,'panel'=4] {'freq'}, dimensions={0} | all-to-all | bytes 204800 | tf_op jit(solution)/shard_map/all_to_all | solution.py:106
  494.5 16.5 %all_to_all.93 = bf16[128,100,1]{1,2,0:T(2,128)(2,1)S(1)} all-to-all(bf16[128,100,1]{1,2,0:T(2,128)(2,1)S(1)} %reshape.640), channel_id=1, replica_groups=mesh['freq'=128,'panel'=4] {'freq'}, dimensions={0} | all-to-all | bytes 51200 | tf_op jit(solution)/shard_map/all_to_all | solution.py:113
  511.2 1.9 multiply_reduce_fusion.4
  513.1 94.5 %psum.73 = f32[]{:T(128)} all-reduce(f32[]{:T(128)} %get-tuple-element.21), channel_id=1, replica_groups=mesh['freq'=128,'panel'=4] {'freq','panel'}, use_global_device_ids=true, to_apply=%region_6.7 | all-reduce | flops 1 | bytes 8 | tf_op jit(solution)/shard_map/psum | solution.py:89
  610.1 19.3 %all_to_all.94 = bf16[128,100,1]{1,2,0:T(2,128)(2,1)S(1)} all-to-all(bf16[128,100,1]{1,2,0:T(2,128)(2,1)S(1)} %copy.53), channel_id=1, replica_groups=mesh['freq'=128,'panel'=4] {'freq'}, dimensions={0} | all-to-all | bytes 51200 | tf_op jit(solution)/shard_map/all_to_all | solution.py:77
  632.3 40.8 %all-reduce.6.cloned.1.call-done = f32[128,400,1]{0,1,2:T(8,128)} async-done(((f32[128,400,1]{0,1,2:T(8,128)}), f32[128,400,1]{0,1,2:T(8,128)}) %all-reduce.6.cloned.1.call-update) | async-done | bytes 204816 | tf_op jit(solution)/shard_map/psum | solution.py:73
  674.2 31.4 %all_to_all.95 = f32[128,400,1]{1,2,0:T(1,128)} all-to-all(f32[128,400,1]{1,2,0:T(1,128)S(1)} %copy.58), channel_id=1, replica_groups=mesh['freq'=128,'panel'=4] {'freq'}, dimensions={0} | all-to-all | bytes 409600 | tf_op jit(solution)/shard_map/all_to_all | solution.py:83
  706.7 2.9 multiply_reduce_fusion.1
  709.7 247.2 %psum.75 = f32[]{:T(128)} all-reduce(f32[]{:T(128)} %get-tuple-element.23), channel_id=1, replica_groups=mesh['freq'=128,'panel'=4] {'freq'}, use_global_device_ids=true, to_apply=%region_9.10 | all-reduce | flops 1 | bytes 8 | tf_op jit(solution)/shard_map/psum | solution.py:92
  957.6 1.8 convolution_convert_fusion.1
  961.2 19.2 %all_to_all.96 = bf16[128,2,200]{2,1,0:T(2,128)(2,1)S(1)} all-to-all(bf16[128,2,200]{2,1,0:T(2,128)(2,1)S(1)} %reshape.645), channel_id=1, replica_groups=mesh['freq'=128,'panel'=4] {'freq'}, dimensions={0} | all-to-all | bytes 204800 | tf_op jit(solution)/shard_map/all_to_all | solution.py:106
  985.5 16.5 %all_to_all.97 = bf16[128,100,1]{1,2,0:T(2,128)(2,1)S(1)} all-to-all(bf16[128,100,1]{1,2,0:T(2,128)(2,1)S(1)} %reshape.641), channel_id=1, replica_groups=mesh['freq'=128,'panel'=4] {'freq'}, dimensions={0} | all-to-all | bytes 51200 | tf_op jit(solution)/shard_map/all_to_all | solution.py:113
  1002.1 1.9 multiply_reduce_fusion.3
  1004.1 94.5 %psum.76 = f32[]{:T(128)} all-reduce(f32[]{:T(128)} %get-tuple-element.25), channel_id=1, replica_groups=mesh['freq'=128,'panel'=4] {'freq','panel'}, use_global_device_ids=true, to_apply=%region_11.12 | all-reduce | flops 1 | bytes 8 | tf_op jit(solution)/shard_map/psum | solution.py:89
  1101.0 19.3 %all_to_all.98 = bf16[128,100,1]{1,2,0:T(2,128)(2,1)S(1)} all-to-all(bf16[128,100,1]{1,2,0:T(2,128)(2,1)S(1)} %copy.69), channel_id=1, replica_groups=mesh['freq'=128,'panel'=4] {'freq'}, dimensions={0} | all-to-all | bytes 51200 | tf_op jit(solution)/shard_map/all_to_all | solution.py:77
  1123.1 40.9 %all-reduce.8.cloned.1.call-done = f32[128,400,1]{0,1,2:T(8,128)} async-done(((f32[128,400,1]{0,1,2:T(8,128)}), f32[128,400,1]{0,1,2:T(8,128)}) %all-reduce.8.cloned.1.call-update) | async-done | bytes 204816 | tf_op jit(solution)/shard_map/psum | solution.py:73
  1165.1 31.6 %all_to_all.99 = f32[128,400,1]{1,2,0:T(1,128)} all-to-all(f32[128,400,1]{1,2,0:T(1,128)S(1)} %copy.74), channel_id=1, replica_groups=mesh['freq'=128,'panel'=4] {'freq'}, dimensions={0} | all-to-all | bytes 409600 | tf_op jit(solution)/shard_map/all_to_all | solution.py:83
  1197.9 3.1 multiply_reduce_fusion
  1201.0 247.0 %psum.78 = f32[]{:T(128)} all-reduce(f32[]{:T(128)} %get-tuple-element.27), channel_id=1, replica_groups=mesh['freq'=128,'panel'=4] {'freq'}, use_global_device_ids=true, to_apply=%region_14.15 | all-reduce | flops 1 | bytes 8 | tf_op jit(solution)/shard_map/psum | solution.py:92
  1452.3 19.2 %all_to_all.100 = bf16[128,2,200]{2,1,0:T(2,128)(2,1)S(1)} all-to-all(bf16[128,2,200]{2,1,0:T(2,128)(2,1)S(1)} %reshape.647), channel_id=1, replica_groups=mesh['freq'=128,'panel'=4] {'freq'}, dimensions={0} | all-to-all | bytes 204800 | tf_op jit(solution)/shard_map/all_to_all | solution.py:106
  1477.2 5.5 all-to-all-start.11
  1483.1 11.1 all-to-all-done.11
  1494.4 2.0 fusion.93
  1496.4 94.5 %psum.79 = f32[]{:T(128)} all-reduce(f32[]{:T(128)} %fusion.93), channel_id=1, replica_groups=mesh['freq'=128,'panel'=4] {'freq','panel'}, use_global_device_ids=true, to_apply=%region_16.17 | all-reduce | flops 1 | bytes 8 | tf_op jit(solution)/shard_map/psum | solution.py:89
  1591.7 2.1 multiply_add_fusion
  (157 shorter events, 47.6 us)
Async XLA Ops:
  6.5 134.8 %copy-start = (bf16[2,1,400,1600]{3,2,1,0:T(8,128)(2,1)S(1)}, bf16[2,1,400,1600]{3,2,1,0:T(8,128)(2,1)}, u32[]{:S(2)}) copy-start(bf16[2,1,400,1600]{3,2,1,0:T(8,128)(2,1)} %param.2) | copy-start | bytes 7680004
  6.5 177.0 %all-reduce.4.cloned.1.call-start = ((), (), s32[]{:S(2)}) async-start(), calls=%async_computation.12 | async-start | bytes 409600 | tf_op jit(solution)/shard_map/psum | solution.py:73
  116.3 0.7 copy-start.7
  116.3 25.6 %copy-start.1 = (f32[1,128,512]{2,1,0:T(8,128)}, f32[1,128,512]{2,1,0:T(8,128)S(1)}, u32[]{:S(2)}) copy-start(f32[1,128,512]{2,1,0:T(8,128)S(1)} %get-tuple-element.17) | copy-start | bytes 786436
  143.3 529.8 %all-reduce.6.cloned.1.call-start = ((), (), s32[]{:S(2)}) async-start(), calls=%async_computation.13 | async-start | bytes 409600 | tf_op jit(solution)/shard_map/psum | solution.py:73
  491.2 20.0 %copy-start.2 = (f32[1,128,512]{2,1,0:T(8,128)S(1)}, f32[1,128,512]{2,1,0:T(8,128)}, u32[]{:S(2)}) copy-start(f32[1,128,512]{2,1,0:T(8,128)} %copy-done.1) | copy-start | bytes 786436
  513.1 117.7 %copy-start.9 = (f32[50,512]{1,0:T(8,128)}, f32[50,512]{1,0:T(8,128)S(1)}, u32[]{:S(2)}) copy-start(f32[50,512]{1,0:T(8,128)S(1)} %get-tuple-element.22) | copy-start | bytes 307204
  632.2 531.8 %all-reduce.8.cloned.1.call-start = ((), (), s32[]{:S(2)}) async-start(), calls=%async_computation.14 | async-start | bytes 409600 | tf_op jit(solution)/shard_map/psum | solution.py:73
  705.6 252.0 %copy-start.3 = (f32[1,128,512]{2,1,0:T(8,128)S(1)}, f32[1,128,512]{2,1,0:T(8,128)}, u32[]{:S(2)}) copy-start(f32[1,128,512]{2,1,0:T(8,128)} %copy-done.1) | copy-start | bytes 786436
  982.1 20.0 %copy-start.4 = (f32[1,128,512]{2,1,0:T(8,128)S(1)}, f32[1,128,512]{2,1,0:T(8,128)}, u32[]{:S(2)}) copy-start(f32[1,128,512]{2,1,0:T(8,128)} %copy-done.1) | copy-start | bytes 786436
  1004.1 117.7 %copy-start.8 = (f32[50,512]{1,0:T(8,128)}, f32[50,512]{1,0:T(8,128)S(1)}, u32[]{:S(2)}) copy-start(f32[50,512]{1,0:T(8,128)S(1)} %get-tuple-element.26) | copy-start | bytes 307204
  1196.8 251.9 %copy-start.5 = (f32[1,128,512]{2,1,0:T(8,128)S(1)}, f32[1,128,512]{2,1,0:T(8,128)}, u32[]{:S(2)}) copy-start(f32[1,128,512]{2,1,0:T(8,128)} %copy-done.1) | copy-start | bytes 786436
  1473.2 21.2 %copy-start.6 = (f32[1,128,512]{2,1,0:T(8,128)S(1)}, f32[1,128,512]{2,1,0:T(8,128)}, u32[]{:S(2)}) copy-start(f32[1,128,512]{2,1,0:T(8,128)} %copy-done.1) | copy-start | bytes 786436
  1477.2 17.1 %all-to-all-start.11 = ((bf16[128,100,1]{1,2,0:T(2,128)(2,1)}), bf16[128,100,1]{1,2,0:T(2,128)(2,1)S(1)}, u32[]{:S(2)}, u32[]{:S(2)}) async-start(bf16[128,100,1]{1,2,0:T(2,128)(2,1)} %reshape.642), calls=%async_computation.11 | async-start | bytes 131072 | tf_op jit(solution)/shard_map/all_to_all | solution.py:113
Sparse Core Ops, SparseCore 0:
  143.4 40.0 all-reduce.3
  632.4 40.7 all-reduce.5
  1123.3 40.7 all-reduce.7
where the time goes:
time: 1610 us; the launch traced here: 1600 us
  blocking collectives  1380 us (86%)
  waiting for transfers between devices  133 us (8%)
  matrix products  34.4 us (2%)
  local copies, waits for them, and re-layouts  23 us (1%)
  between operations  19.3 us (1%)
    psum x3, blocking collectives, model_norm(): return jnp.sqrt(lax.psum(jnp.sum(field * field), 'freq') + epsilon)  741 us
    psum x4, blocking collectives, data_norm(): lax.psum(jnp.sum(field * field), ('freq', 'panel')) + epsilon  390 us
    psum x3, waiting for transfers between devices, summed_panels(): return lax.psum(partial_sum, 'panel')  122 us
    all_to_all x3, blocking collectives, adjoint(): lax.all_to_all(trace_layout(total, blocks), 'freq', split_axis=0, concat_...  94.4 us
    all_to_all x3, blocking collectives, adjoint(): lax.all_to_all(lines, 'freq', split_axis=0, concat_axis=0, tiled=True)  59.1 us
    all_to_all x3, blocking collectives, on_device(): lax.all_to_all(forward_lines, 'freq', split_axis=0, concat_axis=0, tiled=...  57.7 us
    all_to_all x2, blocking collectives, on_device(): lax.all_to_all(trace_layout(product, blocks), 'freq', split_axis=0, conca...  33 us
  transfers between devices with their start and end apart: 4, of which 4 were waited for; matrix products, arithmetic and copies ran while one was open for 0% of the time, Pallas kernels for 0%

commit v1 on v0

--- a/solution.py
+++ b/solution.py
@@ -70,7 +70,7 @@
     table = transform_tables(freq_total, samples)
 
     def summed_panels(partial_sum):
-        return lax.psum(partial_sum, "panel")
+        return jnp.sum(lax.all_gather(partial_sum, "panel"), axis=0)
 
     def adjoint(data):
         lines = spectrum_flat(data, table).astype(jnp.bfloat16)

time: 1610 us -> 1480 us (0.919)
  waiting for transfers between devices: 133 us -> 11.1 us
    psum x3 -> x0, waiting for transfers between devices: 122 us -> none  [summed_panels(): return lax.psum(partial_sum, 'panel')]
    all_gather x0 -> x3, blocking collectives: none -> 33.5 us  [summed_panels(): return jnp.sum(lax.all_gather(partial_sum, 'panel'), axis=0)]
    all_to_all x3, blocking collectives: 94.4 us -> 72 us  [adjoint(): lax.all_to_all(trace_layout(total, blocks), 'freq', split_axis=0, concat_...]
  transfers between devices with their start and end apart: 4 -> 1, of which waited for: 4 -> 1; matrix products, arithmetic and copies ran while one was open for 0% -> 0% of each run, Pallas kernels for 0% -> 0%
where the time goes in v1:
time: 1480 us; the launch traced here: 1470 us
  blocking collectives  1390 us (94%)
  matrix products  34.4 us (2%)
  local copies, waits for them, and re-layouts  18.2 us (1%)
    psum x3, blocking collectives, model_norm(): return jnp.sqrt(lax.psum(jnp.sum(field * field), 'freq') + epsilon)  741 us
    psum x4, blocking collectives, data_norm(): lax.psum(jnp.sum(field * field), ('freq', 'panel')) + epsilon  390 us
    all_to_all x3, blocking collectives, adjoint(): lax.all_to_all(trace_layout(total, blocks), 'freq', split_axis=0, concat_...  72 us
    all_to_all x3, blocking collectives, adjoint(): lax.all_to_all(lines, 'freq', split_axis=0, concat_axis=0, tiled=True)  59.1 us
    all_to_all x3, blocking collectives, on_device(): lax.all_to_all(forward_lines, 'freq', split_axis=0, concat_axis=0, tiled=...  57.7 us
    all_gather x3, blocking collectives, summed_panels(): return jnp.sum(lax.all_gather(partial_sum, 'panel'), axis=0)  33.5 us
    all_to_all x2, blocking collectives, on_device(): lax.all_to_all(trace_layout(product, blocks), 'freq', split_axis=0, conca...  33 us
  transfers between devices with their start and end apart: 1, of which 1 were waited for; matrix products, arithmetic and copies ran while one was open for 0% of the time, Pallas kernels for 0%

profile of v1, /device:TPU:1, one launch (start us, length us, event | category | flops | bytes accessed | tf_op | source)
XLA Modules:
  0.0 1471.8 jit_solution(6590953463883659366)
XLA Ops:
  0.0 1.9 multiply_reduce_fusion.5
  1.9 106.0 %psum.49 = f32[]{:T(128)} all-reduce(f32[]{:T(128)} %multiply_reduce_fusion.5), channel_id=1, replica_groups=mesh['freq'=128,'panel'=4] {'freq','panel'}, use_global_device_ids=true, to_apply=%region_1.2 | all-reduce | flops 1 | bytes 8 | tf_op jit(solution)/shard_map/psum | solution.py:89
  112.1 20.5 %all_to_all.90 = bf16[128,100,1]{1,2,0:T(2,128)(2,1)S(1)} all-to-all(bf16[128,100,1]{1,2,0:T(2,128)(2,1)S(1)} %copy.34), channel_id=1, replica_groups=mesh['freq'=128,'panel'=4] {'freq'}, dimensions={0} | all-to-all | bytes 51200 | tf_op jit(solution)/shard_map/all_to_all | solution.py:77
  135.7 11.0 all-gather
  147.2 23.8 %all_to_all.91 = f32[128,400,1]{1,2,0:T(1,128)S(1)} all-to-all(f32[128,400,1]{1,2,0:T(1,128)S(1)} %copy.39), channel_id=1, replica_groups=mesh['freq'=128,'panel'=4] {'freq'}, dimensions={0} | all-to-all | bytes 409600 | tf_op jit(solution)/shard_map/all_to_all | solution.py:83
  171.2 2.2 multiply_reduce_fusion.2
  173.4 247.2 %psum.50 = f32[]{:T(128)} all-reduce(f32[]{:T(128)} %get-tuple-element.19), channel_id=1, replica_groups=mesh['freq'=128,'panel'=4] {'freq'}, use_global_device_ids=true, to_apply=%region_4.5 | all-reduce | flops 1 | bytes 8 | tf_op jit(solution)/shard_map/psum | solution.py:92
  425.4 19.2 %all_to_all.92 = bf16[128,2,200]{2,1,0:T(2,128)(2,1)S(1)} all-to-all(bf16[128,2,200]{2,1,0:T(2,128)(2,1)S(1)} %reshape.655), channel_id=1, replica_groups=mesh['freq'=128,'panel'=4] {'freq'}, dimensions={0} | all-to-all | bytes 204800 | tf_op jit(solution)/shard_map/all_to_all | solution.py:106
  449.6 16.5 %all_to_all.93 = bf16[128,100,1]{1,2,0:T(2,128)(2,1)S(1)} all-to-all(bf16[128,100,1]{1,2,0:T(2,128)(2,1)S(1)} %reshape.652), channel_id=1, replica_groups=mesh['freq'=128,'panel'=4] {'freq'}, dimensions={0} | all-to-all | bytes 51200 | tf_op jit(solution)/shard_map/all_to_all | solution.py:113
  466.3 1.9 multiply_reduce_fusion.4
  468.2 94.0 %psum.51 = f32[]{:T(128)} all-reduce(f32[]{:T(128)} %get-tuple-element.21), channel_id=1, replica_groups=mesh['freq'=128,'panel'=4] {'freq','panel'}, use_global_device_ids=true, to_apply=%region_6.7 | all-reduce | flops 1 | bytes 8 | tf_op jit(solution)/shard_map/psum | solution.py:89
  564.6 19.3 %all_to_all.94 = bf16[128,100,1]{1,2,0:T(2,128)(2,1)S(1)} all-to-all(bf16[128,100,1]{1,2,0:T(2,128)(2,1)S(1)} %copy.50), channel_id=1, replica_groups=mesh['freq'=128,'panel'=4] {'freq'}, dimensions={0} | all-to-all | bytes 51200 | tf_op jit(solution)/shard_map/all_to_all | solution.py:77
  585.8 11.6 all-gather.1
  597.9 23.3 %all_to_all.95 = f32[128,400,1]{1,2,0:T(1,128)} all-to-all(f32[128,400,1]{1,2,0:T(1,128)S(1)} %copy.55), channel_id=1, replica_groups=mesh['freq'=128,'panel'=4] {'freq'}, dimensions={0} | all-to-all | bytes 409600 | tf_op jit(solution)/shard_map/all_to_all | solution.py:83
  622.3 3.0 multiply_reduce_fusion.1
  625.2 247.2 %psum.52 = f32[]{:T(128)} all-reduce(f32[]{:T(128)} %get-tuple-element.23), channel_id=1, replica_groups=mesh['freq'=128,'panel'=4] {'freq'}, use_global_device_ids=true, to_apply=%region_9.10 | all-reduce | flops 1 | bytes 8 | tf_op jit(solution)/shard_map/psum | solution.py:92
  876.8 19.2 %all_to_all.96 = bf16[128,2,200]{2,1,0:T(2,128)(2,1)S(1)} all-to-all(bf16[128,2,200]{2,1,0:T(2,128)(2,1)S(1)} %reshape.657), channel_id=1, replica_groups=mesh['freq'=128,'panel'=4] {'freq'}, dimensions={0} | all-to-all | bytes 204800 | tf_op jit(solution)/shard_map/all_to_all | solution.py:106
  901.0 16.5 %all_to_all.97 = bf16[128,100,1]{1,2,0:T(2,128)(2,1)S(1)} all-to-all(bf16[128,100,1]{1,2,0:T(2,128)(2,1)S(1)} %reshape.653), channel_id=1, replica_groups=mesh['freq'=128,'panel'=4] {'freq'}, dimensions={0} | all-to-all | bytes 51200 | tf_op jit(solution)/shard_map/all_to_all | solution.py:113
  917.7 2.0 multiply_reduce_fusion.3
  919.6 95.4 %psum.53 = f32[]{:T(128)} all-reduce(f32[]{:T(128)} %get-tuple-element.25), channel_id=1, replica_groups=mesh['freq'=128,'panel'=4] {'freq','panel'}, use_global_device_ids=true, to_apply=%region_11.12 | all-reduce | flops 1 | bytes 8 | tf_op jit(solution)/shard_map/psum | solution.py:89
  1017.5 19.3 %all_to_all.98 = bf16[128,100,1]{1,2,0:T(2,128)(2,1)S(1)} all-to-all(bf16[128,100,1]{1,2,0:T(2,128)(2,1)S(1)} %copy.66), channel_id=1, replica_groups=mesh['freq'=128,'panel'=4] {'freq'}, dimensions={0} | all-to-all | bytes 51200 | tf_op jit(solution)/shard_map/all_to_all | solution.py:77
  1038.6 11.0 all-gather.2
  1050.1 24.9 %all_to_all.99 = f32[128,400,1]{1,2,0:T(1,128)} all-to-all(f32[128,400,1]{1,2,0:T(1,128)S(1)} %copy.71), channel_id=1, replica_groups=mesh['freq'=128,'panel'=4] {'freq'}, dimensions={0} | all-to-all | bytes 409600 | tf_op jit(solution)/shard_map/all_to_all | solution.py:83
  1076.2 3.0 multiply_reduce_fusion
  1079.2 247.0 %psum.54 = f32[]{:T(128)} all-reduce(f32[]{:T(128)} %get-tuple-element.27), channel_id=1, replica_groups=mesh['freq'=128,'panel'=4] {'freq'}, use_global_device_ids=true, to_apply=%region_14.15 | all-reduce | flops 1 | bytes 8 | tf_op jit(solution)/shard_map/psum | solution.py:92
  1327.0 1.8 convolution_convert_fusion
  1330.6 19.2 %all_to_all.100 = bf16[128,2,200]{2,1,0:T(2,128)(2,1)S(1)} all-to-all(bf16[128,2,200]{2,1,0:T(2,128)(2,1)S(1)} %reshape.659), channel_id=1, replica_groups=mesh['freq'=128,'panel'=4] {'freq'}, dimensions={0} | all-to-all | bytes 204800 | tf_op jit(solution)/shard_map/all_to_all | solution.py:106
  1355.4 5.6 all-to-all-start.11
  1361.4 11.1 all-to-all-done.11
  1372.7 2.0 fusion.93
  1374.7 94.0 %psum.55 = f32[]{:T(128)} all-reduce(f32[]{:T(128)} %fusion.93), channel_id=1, replica_groups=mesh['freq'=128,'panel'=4] {'freq','panel'}, use_global_device_ids=true, to_apply=%region_16.17 | all-reduce | flops 1 | bytes 8 | tf_op jit(solution)/shard_map/psum | solution.py:89
  1469.5 2.1 multiply_add_fusion
  (154 shorter events, 42.8 us)
Async XLA Ops:
  0.0 134.8 %copy-start = (bf16[2,1,400,1600]{3,2,1,0:T(8,128)(2,1)S(1)}, bf16[2,1,400,1600]{3,2,1,0:T(8,128)(2,1)}, u32[]{:S(2)}) copy-start(bf16[2,1,400,1600]{3,2,1,0:T(8,128)(2,1)} %param.2) | copy-start | bytes 7680004
  109.7 0.7 copy-start.7
  109.7 25.7 %copy-start.1 = (f32[1,128,512]{2,1,0:T(8,128)}, f32[1,128,512]{2,1,0:T(8,128)S(1)}, u32[]{:S(2)}) copy-start(f32[1,128,512]{2,1,0:T(8,128)S(1)} %get-tuple-element.17) | copy-start | bytes 786436
  446.3 20.0 %copy-start.2 = (f32[1,128,512]{2,1,0:T(8,128)S(1)}, f32[1,128,512]{2,1,0:T(8,128)}, u32[]{:S(2)}) copy-start(f32[1,128,512]{2,1,0:T(8,128)} %copy-done.1) | copy-start | bytes 786436
  468.2 117.2 %copy-start.9 = (f32[50,512]{1,0:T(8,128)}, f32[50,512]{1,0:T(8,128)S(1)}, u32[]{:S(2)}) copy-start(f32[50,512]{1,0:T(8,128)S(1)} %get-tuple-element.22) | copy-start | bytes 307204
  621.1 252.0 %copy-start.3 = (f32[1,128,512]{2,1,0:T(8,128)S(1)}, f32[1,128,512]{2,1,0:T(8,128)}, u32[]{:S(2)}) copy-start(f32[1,128,512]{2,1,0:T(8,128)} %copy-done.1) | copy-start | bytes 786436
  897.7 20.0 %copy-start.4 = (f32[1,128,512]{2,1,0:T(8,128)S(1)}, f32[1,128,512]{2,1,0:T(8,128)}, u32[]{:S(2)}) copy-start(f32[1,128,512]{2,1,0:T(8,128)} %copy-done.1) | copy-start | bytes 786436
  919.6 118.7 %copy-start.8 = (f32[50,512]{1,0:T(8,128)}, f32[50,512]{1,0:T(8,128)S(1)}, u32[]{:S(2)}) copy-start(f32[50,512]{1,0:T(8,128)S(1)} %get-tuple-element.26) | copy-start | bytes 307204
  1075.1 251.9 %copy-start.5 = (f32[1,128,512]{2,1,0:T(8,128)S(1)}, f32[1,128,512]{2,1,0:T(8,128)}, u32[]{:S(2)}) copy-start(f32[1,128,512]{2,1,0:T(8,128)} %copy-done.1) | copy-start | bytes 786436
  1351.5 21.2 %copy-start.6 = (f32[1,128,512]{2,1,0:T(8,128)S(1)}, f32[1,128,512]{2,1,0:T(8,128)}, u32[]{:S(2)}) copy-start(f32[1,128,512]{2,1,0:T(8,128)} %copy-done.1) | copy-start | bytes 786436
  1355.4 17.1 %all-to-all-start.11 = ((bf16[128,100,1]{1,2,0:T(2,128)(2,1)}), bf16[128,100,1]{1,2,0:T(2,128)(2,1)S(1)}, u32[]{:S(2)}, u32[]{:S(2)}) async-start(bf16[128,100,1]{1,2,0:T(2,128)(2,1)} %reshape.654), calls=%async_computation.11 | async-start | bytes 131072 | tf_op jit(solution)/shard_map/all_to_all | solution.py:113
